TPU v7x, 512 devices: a whole 4x4x16 slice. The times are simulated.
512 devices in a mesh: rep: 4 (over x), rows: 128 (over y, z, core).
Axes of the slice: x: 4, y: 4, z: 16, core: 2. Of those that a mesh axis runs over, the one named last changes fastest.
Arguments:
- features: bfloat16 [65536, 256], P('rows'), may hold values from -6 to 6
- tiles: bfloat16 [128, 4, 2, 256, 256], P('rows', 'rep'), may hold values from -0.1875 to 0.1875
- tile_row: int32 [128, 4, 2], P('rows', 'rep'), may hold values from 0 to 1, as said below
- tile_col: int32 [128, 4, 2], P('rows', 'rep'), may hold values from 0 to 3, as said below
- tile_live: int32 [128, 4], P('rows', 'rep'), may hold values from 1 to 2, as said below
- send_index: int32 [128, 128, 4], P('rows'), may hold values from 0 to 511
- gain: float32 [3, 256], replicated, may hold values from 0.1 to 1.9
- w_in: bfloat16 [3, 256, 512], replicated, may hold values from -0.375 to 0.375
- w_out: bfloat16 [3, 512, 256], replicated, may hold values from -0.25 to 0.25
Outputs:
- result: bfloat16 [65536, 256], P('rows')
Inputs may be any that keep to these rules, and one draw needn't show every extreme that they name: `tile_live`: every owner and section has at least one slot in use, and some owner and section has all 2. For each owner, the pairs (tile_row, tile_col) over all sections and slots are all different. For each owner, the pairs (tile_row, tile_col) over all sections and slots are all different.
All inputs are finite; a program needn't handle non-finite values.
Results may differ from a plain program's by a relative error of at most 0.012.
Values may be sent and summed in bfloat16 or wider, within the bound.
A program may use at most 64 MiB of HBM per device.

v0:
```python
import jax
import jax.numpy as jnp
from jax import lax
from jax.sharding import PartitionSpec as P

HOPS = 3


def update_rows(current_rows, gathered, gain_row, first, second):
    mixed = current_rows.astype(jnp.float32) + gathered
    scale = lax.rsqrt(jnp.mean(mixed * mixed, axis=-1, keepdims=True) + 1e-06)
    normed = (mixed * scale * gain_row[None, :]).astype(jnp.bfloat16)
    inner = jax.nn.gelu(jnp.dot(normed, first, preferred_element_type=jnp.float32)).astype(
        jnp.bfloat16
    )
    return (mixed + jnp.dot(inner, second, preferred_element_type=jnp.float32)).astype(jnp.bfloat16)


def per_device(features, tiles, tile_row, tile_col, tile_live, send_index, gain, w_in, w_out):
    owners = lax.axis_size("rows")
    nodes = features.shape[0]
    width = features.shape[1]
    tile_side = tiles.shape[-1]
    slots = tiles.shape[2]
    halo_width = send_index.shape[2]
    halo_pad = (owners * halo_width + tile_side - 1) // tile_side * tile_side
    row_tiles = nodes // tile_side
    col_tiles = (nodes + halo_pad) // tile_side
    my_tiles = tiles[0, 0]
    slot_live = (jnp.arange(slots, dtype=jnp.int32) < tile_live[0, 0]).astype(jnp.float32)
    onehot = (tile_row[0, 0][:, None] == jnp.arange(row_tiles, dtype=jnp.int32)[None, :]).astype(
        jnp.float32
    )
    onehot = onehot * slot_live[:, None]
    pad_rows = jnp.zeros((halo_pad - owners * halo_width, width), jnp.bfloat16)
    current = features
    for step in range(HOPS):
        outgoing = current[send_index[0]]
        incoming = lax.all_to_all(outgoing, "rows", split_axis=0, concat_axis=0, tiled=True)
        extended = jnp.concatenate(
            [current, incoming.reshape(owners * halo_width, width), pad_rows], axis=0
        )
        picked = extended.reshape(col_tiles, tile_side, width)[tile_col[0, 0]]
        products = jnp.einsum("tij,tjf->tif", my_tiles, picked, preferred_element_type=jnp.float32)
        partial_value = jnp.einsum("tr,tif->rif", onehot, products).reshape(nodes, width)
        gathered = lax.psum(partial_value, "rep")
        current = update_rows(current, gathered, gain[step], w_in[step], w_out[step])
    return current


def solution(mesh):
    placed = (
        P("rows", None),
        P("rows", "rep", None, None, None),
        P("rows", "rep", None),
        P("rows", "rep", None),
        P("rows", "rep"),
        P("rows", None, None),
        P(),
        P(),
        P(),
    )
    return jax.shard_map(
        per_device, mesh=mesh, in_specs=placed, out_specs=P("rows", None), check_vma=False
    )
```

profile of v0, /device:TPU:1, one launch (start us, length us, event | category | flops | bytes accessed | tf_op | source)
XLA Modules:
  0.0 303.2 jit_solution(10579522859335403321)
XLA Ops:
  6.5 0.7 compare_select_fusion
  7.5 2.5 gather_fusion
  10.1 0.8 reshape.123
  10.8 20.6 %all-to-all-start = ((bf16[128,4,256]{2,1,0:T(4,128)(2,1)}), bf16[128,4,256]{2,1,0:T(4,128)(2,1)S(1)}, u32[]{:S(2)}, u32[]{:S(2)}) async-start(bf16[128,4,256]{2,1,0:T(4,128)(2,1)} %reshape.123), calls=%async_computation | async-start | bytes 524288 | tf_op jit(solution)/shard_map/all_to_all | solution.py:39
  32.1 0.6 copy-done.8
  32.8 21.0 %all-to-all-done = bf16[128,4,256]{2,1,0:T(4,128)(2,1)S(1)} async-done(((bf16[128,4,256]{2,1,0:T(4,128)(2,1)}), bf16[128,4,256]{2,1,0:T(4,128)(2,1)S(1)}, u32[]{:S(2)}, u32[]{:S(2)}) %all-to-all-start) | async-done | bytes 262176 | tf_op jit(solution)/shard_map/all_to_all | solution.py:39
  53.9 0.6 gather_fusion.1
  54.5 0.3 fusion.58
  55.0 0.6 copy-done.9
  55.6 0.4 fusion.31
  56.1 0.8 copy.13
  57.0 0.6 copy-done.5
  57.6 47.2 %all-reduce.4.cloned.1.call-done = f32[512,256]{1,0:T(8,128)} async-done(((f32[512,256]{1,0:T(8,128)}), f32[512,256]{1,0:T(8,128)}) %all-reduce.4.cloned.1.call-update) | async-done | bytes 524304 | tf_op jit(solution)/shard_map/psum | solution.py:46
  104.8 1.3 multiply_reduce_fusion.2
  106.1 0.7 fusion
  106.8 2.0 gather_fusion.2
  108.8 41.0 %all_to_all.15 = bf16[128,4,256]{2,1,0:T(4,128)(2,1)S(1)} all-to-all(bf16[128,4,256]{2,1,0:T(4,128)(2,1)S(1)} %reshape.139), channel_id=1, replica_groups=mesh['rep'=4,'rows'=128] {'rows'}, dimensions={0} | all-to-all | bytes 524288 | tf_op jit(solution)/shard_map/all_to_all | solution.py:39
  150.0 0.6 gather_fusion.3
  150.5 0.3 fusion.56
  151.0 0.4 fusion.29
  151.4 0.8 copy.14
  152.3 47.1 %all-reduce.6.cloned.1.call-done = f32[512,256]{1,0:T(8,128)} async-done(((f32[512,256]{1,0:T(8,128)}), f32[512,256]{1,0:T(8,128)}) %all-reduce.6.cloned.1.call-update) | async-done | bytes 524304 | tf_op jit(solution)/shard_map/psum | solution.py:46
  199.4 1.3 multiply_reduce_fusion.1
  200.7 0.7 fusion.1
  201.4 2.0 gather_fusion.4
  203.4 41.0 %all_to_all.16 = bf16[128,4,256]{2,1,0:T(4,128)(2,1)S(1)} all-to-all(bf16[128,4,256]{2,1,0:T(4,128)(2,1)S(1)} %reshape.155), channel_id=1, replica_groups=mesh['rep'=4,'rows'=128] {'rows'}, dimensions={0} | all-to-all | bytes 524288 | tf_op jit(solution)/shard_map/all_to_all | solution.py:39
  244.6 0.6 gather_fusion.5
  245.6 0.4 fusion.27
  246.0 0.8 copy.15
  246.9 47.1 %all-reduce.8.cloned.1.call-done = f32[512,256]{1,0:T(8,128)} async-done(((f32[512,256]{1,0:T(8,128)}), f32[512,256]{1,0:T(8,128)}) %all-reduce.8.cloned.1.call-update) | async-done | bytes 524304 | tf_op jit(solution)/shard_map/psum | solution.py:46
  294.0 1.3 multiply_reduce_fusion
  295.3 1.4 fusion.2
  (45 shorter events, 1.8 us)
Async XLA Ops:
  6.5 47.9 %copy-start = (bf16[1,1,2,256,256]{4,3,2,1,0:T(8,128)(2,1)S(1)}, bf16[1,1,2,256,256]{4,3,2,1,0:T(8,128)(2,1)}, u32[]{:S(2)}) copy-start(bf16[1,1,2,256,256]{4,3,2,1,0:T(8,128)(2,1)} %param.10) | copy-start | bytes 786436
  10.8 43.0 %all-to-all-start = ((bf16[128,4,256]{2,1,0:T(4,128)(2,1)}), bf16[128,4,256]{2,1,0:T(4,128)(2,1)S(1)}, u32[]{:S(2)}, u32[]{:S(2)}) async-start(bf16[128,4,256]{2,1,0:T(4,128)(2,1)} %reshape.123), calls=%async_computation | async-start | bytes 524288 | tf_op jit(solution)/shard_map/all_to_all | solution.py:39
  31.4 73.4 %all-reduce.4.cloned.1.call-start = ((), (), s32[]{:S(2)}) async-start(), calls=%async_computation.3 | async-start | bytes 1048576 | tf_op jit(solution)/shard_map/psum | solution.py:46
  32.1 0.7 copy-start.8
  32.8 21.1 %copy-start.1 = (bf16[512,256]{1,0:T(8,128)(2,1)S(1)}, bf16[512,256]{1,0:T(8,128)(2,1)}, u32[]{:S(2)}) copy-start(bf16[512,256]{1,0:T(8,128)(2,1)} %param.9) | copy-start | bytes 786436
  55.0 0.7 copy-start.9
  56.0 50.0 %copy-start.6 = (bf16[3,512,256]{2,1,0:T(8,128)(2,1)S(1)}, bf16[3,512,256]{2,1,0:T(8,128)(2,1)}, u32[]{:S(2)}) copy-start(bf16[3,512,256]{2,1,0:T(8,128)(2,1)} %param.17) | copy-start | bytes 2359300
  56.0 50.0 %copy-start.7 = (bf16[3,256,512]{2,1,0:T(8,128)(2,1)S(1)}, bf16[3,256,512]{2,1,0:T(8,128)(2,1)}, u32[]{:S(2)}) copy-start(bf16[3,256,512]{2,1,0:T(8,128)(2,1)} %param.16) | copy-start | bytes 2359300
  56.9 0.7 copy-start.5
  56.9 142.5 %all-reduce.6.cloned.1.call-start = ((), (), s32[]{:S(2)}) async-start(), calls=%async_computation.4 | async-start | bytes 1048576 | tf_op jit(solution)/shard_map/psum | solution.py:46
  104.8 1.3 copy-start.2
  152.3 141.7 %all-reduce.8.cloned.1.call-start = ((), (), s32[]{:S(2)}) async-start(), calls=%async_computation.5 | async-start | bytes 1048576 | tf_op jit(solution)/shard_map/psum | solution.py:46
  199.4 1.3 copy-start.3
  294.0 1.3 copy-start.4
Sparse Core Ops, SparseCore 0:
  57.0 47.7 all-reduce.3
  152.4 46.9 all-reduce.5
  247.0 46.9 all-reduce.7
where the time goes:
time: 305 us; the launch traced here: 303 us
  waiting for transfers between devices  162 us (53%)
  blocking collectives  82.1 us (27%)
  starting transfers between devices  20.7 us (7%)
  local copies, waits for them, and re-layouts  14.5 us (5%)
  between operations  14.1 us (5%)
  matrix products  4.75 us (2%)
  other arithmetic  4.68 us (2%)
    psum x3, waiting for transfers between devices, per_device(): gathered = lax.psum(partial_value, 'rep')  141 us
    all_to_all x2, blocking collectives, per_device(): lax.all_to_all(outgoing, 'rows', split_axis=0, concat_axis=0, tiled=True)  82.1 us
    all_to_all x1, waiting for transfers between devices, per_device(): lax.all_to_all(outgoing, 'rows', split_axis=0, concat_axis=0, tiled=True)  21 us
    all_to_all x1, starting transfers between devices, per_device(): lax.all_to_all(outgoing, 'rows', split_axis=0, concat_axis=0, tiled=True)  20.6 us
    gather x6, local copies, waits for them, and re-layouts, per_device(): outgoing = current[send_index[0]]  7.36 us
  transfers between devices with their start and end apart: 4, of which 4 were waited for; matrix products, arithmetic and copies ran while one was open for 0% of the time, Pallas kernels for 0%

commit v1 on v0

v1 whole, which is shorter than its diff:
```python
import functools

import jax
import jax.numpy as jnp
from jax import lax
from jax.experimental import pallas as pl
from jax.experimental.pallas import tpu as pltpu
from jax.sharding import PartitionSpec as P

HOPS = 3
MESH = pl.DeviceIdType.MESH
BF = jnp.bfloat16
F32 = jnp.float32


def plane_of(owners):
    return {128: (4, 16, 2), 8: (2, 2, 2)}[owners]


def kernel(
    reps, owners, feat_hbm, tiles_hbm, row_ref, col_ref, live_ref, index_ref, gain_ref, win_hbm, wout_hbm,
    out_ref,
    index_t, cur, pick, sent, recv, half_mask, spread, tiles_all, marks, block, wide, total, win, wout,
    load_sem, tile_send, tile_recv, mark_send, mark_recv, halo_send, halo_recv, own_sem,
):
    ys, zs, cs = plane_of(owners)
    rep = lax.axis_index("rep")
    me = lax.axis_index("rows")
    my_y, my_z, my_c = me // (zs * cs), (me // cs) % zs, me % cs
    nodes, width = feat_hbm.shape
    side = tiles_hbm.shape[-1]
    slots = tiles_hbm.shape[0]
    halo = index_ref.shape[0]
    half = width // 2
    group = 2 * halo
    row_tiles = nodes // side
    col_tiles = block.shape[1] // side
    own_tiles = nodes // side

    barrier = pltpu.get_barrier_semaphore()

    def target(dz, dy, dc):
        y = lax.rem(my_y + dy, ys)
        z = lax.rem(my_z + dz, zs)
        c = lax.rem(my_c + dc, cs)
        return (y * zs + z) * cs + c

    def far_first(visit):
        def some(dz, skip_self):
            for dy in sorted(range(ys), key=lambda d: -min(d, ys - d)):
                for dc in reversed(range(cs)):
                    if skip_self and dy == 0 and dc == 0:
                        continue
                    visit(target(dz, dy, dc))

        @pl.loop(0, zs - 1)
        def _(j):
            some(zs // 2 + (1 - 2 * lax.rem(j, 2)) * ((j + 1) // 2), False)

        some(0, True)

    def greet(owner):
        pl.semaphore_signal(barrier, inc=1, device_id=(rep, owner), device_id_type=MESH)

    far_first(greet)
    for d in range(1, reps):
        pl.semaphore_signal(
            barrier, inc=1, device_id=(lax.rem(rep + d, reps), me), device_id_type=MESH
        )

    loads = [
        pltpu.make_async_copy(feat_hbm, cur, load_sem.at[0]),
        pltpu.make_async_copy(tiles_hbm, tiles_all.at[rep], load_sem.at[1]),
        pltpu.make_async_copy(win_hbm, win, load_sem.at[2]),
        pltpu.make_async_copy(wout_hbm, wout, load_sem.at[3]),
    ]
    for load in loads:
        load.start()

    positions = row_tiles * col_tiles
    line = lax.broadcasted_iota(jnp.int32, marks.shape[1:], 0)
    mark = jnp.zeros(marks.shape[1:], F32)
    for slot in range(slots):
        where = row_ref[slot] * col_tiles + col_ref[slot]
        where = jnp.where(slot < live_ref[0], where + slot * positions, -1)
        mark = jnp.where(line == where, 1.0, mark)
    marks[rep] = mark

    per = 16 // group
    wide_index = jnp.concatenate([index_ref[...]] * 2, axis=0)
    index_t[...] = jnp.transpose(wide_index)
    lane = lax.broadcasted_iota(jnp.int32, (group, group), 1)
    sub = lax.broadcasted_iota(jnp.int32, (group, group), 0)
    node = lax.broadcasted_iota(jnp.int32, (group, nodes), 1)
    for o in range(0, owners, per):
        rows = []
        for q in range(per):
            wanted = jnp.broadcast_to(index_t[o + q : o + q + 1, :], (group, group))
            wanted = jnp.sum(jnp.where(lane == sub, wanted, 0), axis=1, keepdims=True)
            rows.append(jnp.where(node == wanted, 1.0, 0.0).astype(F32))
        pick[o * group : (o + per) * group, :] = jnp.concatenate(rows, axis=0).astype(BF)
    total_lines = owners * group
    lines = lax.broadcasted_iota(jnp.int32, (total_lines, half), 0)
    half_mask[...] = jnp.where(lax.rem(lines, group) < halo, 1.0, 0.0).astype(BF)
    at = lax.broadcasted_iota(jnp.int32, spread.shape, 0)
    to = lax.broadcasted_iota(jnp.int32, spread.shape, 1)
    same = (at // halo == to // group) & (lax.rem(at, halo) == lax.rem(to, halo))
    spread[...] = jnp.where(same, 1.0, 0.0).astype(BF)

    loads[0].wait()

    def gather(hop):
        step = min(256, total_lines)
        for first in range(0, total_lines, step):
            got = jnp.dot(pick[first : first + step, :], cur[...], preferred_element_type=F32)
            line = lax.rem(lax.broadcasted_iota(jnp.int32, (step, half), 0), group)
            message = jnp.where(line < halo, got[:, :half], got[:, half:])
            sent[hop, first // group : (first + step) // group] = message.astype(BF).reshape(
                step // group, group, half
            )

    def exchange(hop):
        def send(owner):
            pltpu.make_async_remote_copy(
                src_ref=sent.at[hop, owner],
                dst_ref=recv.at[hop, me],
                send_sem=halo_send.at[hop],
                recv_sem=halo_recv.at[hop],
                device_id=(rep, owner),
                device_id_type=MESH,
            ).start()

        far_first(send)
        pltpu.make_async_copy(sent.at[hop, me], recv.at[hop, me], own_sem.at[hop]).start()

    gather(0)
    pl.semaphore_wait(barrier, owners - 1 + reps - 1)
    exchange(0)
    for d in range(1, reps):
        peer = (lax.rem(rep + d, reps), me)
        pltpu.make_async_remote_copy(
            src_ref=marks.at[rep], dst_ref=marks.at[rep], send_sem=mark_send, recv_sem=mark_recv,
            device_id=peer, device_id_type=MESH,
        ).start()
        pltpu.make_async_remote_copy(
            src_ref=tiles_hbm, dst_ref=tiles_all.at[rep], send_sem=tile_send, recv_sem=tile_recv,
            device_id=peer, device_id_type=MESH,
        ).start()

    for load in loads[1:]:
        load.wait()
    others = pl.ds(0, reps - 1)
    pltpu.make_async_copy(marks.at[others], marks.at[others], mark_recv).wait()
    pltpu.make_async_copy(tiles_all.at[others], tiles_all.at[others], tile_recv).wait()

    chunk = 64
    for r in range(row_tiles):
        for c in range(col_tiles):

            @pl.loop(0, side // chunk)
            def _(i):
                at = pl.ds(pl.multiple_of(i * chunk, chunk), chunk)
                to = pl.ds(pl.multiple_of(r * side + i * chunk, chunk), chunk)
                value = jnp.zeros((chunk, side), F32)
                for s in range(reps):
                    for slot in range(slots):
                        which = slot * positions + r * col_tiles + c
                        here = marks[s, which : which + 1, :]
                        here = jnp.concatenate([here] * (side // here.shape[1]), axis=1)
                        value += tiles_all[s, slot, at, :].astype(F32) * here
                block[to, c * side : (c + 1) * side] = value.astype(BF)

    for c in range(own_tiles, col_tiles):
        q = c - own_tiles
        columns = min(2 * side, wide.shape[1])
        wide[:, q * 2 * side : q * 2 * side + columns] = jnp.dot(
            block[:, c * side : (c + 1) * side], spread[:, :columns], preferred_element_type=F32
        ).astype(BF)

    rows = 256
    for hop in range(HOPS):
        if hop:
            gather(hop)
            exchange(hop)
        for first in range(0, nodes, rows):
            total[first : first + rows, :] = jnp.dot(
                block[first : first + rows, :nodes], cur[...], preferred_element_type=F32
            ) + cur[first : first + rows, :].astype(F32)
        pltpu.make_async_copy(sent.at[hop, me], recv.at[hop, me], own_sem.at[hop]).wait()
        arrived = recv.at[hop, pl.ds(0, owners - 1)]
        pltpu.make_async_copy(arrived, arrived, halo_recv.at[hop]).wait()
        came = recv[hop].reshape(total_lines, half)
        low = came * half_mask[...]
        both = jnp.concatenate([low, came - low], axis=1)
        for first in range(0, nodes, rows):
            here = slice(first, first + rows)
            mixed = total[here, :] + jnp.dot(wide[here, :], both, preferred_element_type=F32)
            scale = lax.rsqrt(jnp.mean(mixed * mixed, axis=-1, keepdims=True) + 1e-06)
            normed = (mixed * scale * gain_ref[hop : hop + 1, :]).astype(BF)
            inner = jax.nn.gelu(jnp.dot(normed, win[hop], preferred_element_type=F32)).astype(BF)
            result = (mixed + jnp.dot(inner, wout[hop], preferred_element_type=F32)).astype(BF)
            if hop == HOPS - 1:
                out_ref[here, :] = result
            else:
                cur[here, :] = result

    for hop in range(HOPS):
        left = sent.at[hop, pl.ds(0, owners - 1)]
        pltpu.make_async_copy(left, left, halo_send.at[hop]).wait()
    pltpu.make_async_copy(marks.at[others], marks.at[others], mark_send).wait()
    pltpu.make_async_copy(tiles_all.at[others], tiles_all.at[others], tile_send).wait()


def per_device(reps, owners, features, tiles, tile_row, tile_col, tile_live, send_index, gain, w_in, w_out):
    nodes, width = features.shape
    slots, side = tiles.shape[2], tiles.shape[-1]
    halo = send_index.shape[2]
    halo_pad = (owners * halo + side - 1) // side * side
    columns = nodes + halo_pad
    lines = owners * 2 * halo
    positions = (nodes // side) * (columns // side)
    mark_lines = (slots * positions + 7) // 8 * 8
    smem = pl.BlockSpec(memory_space=pltpu.SMEM)
    vmem = pl.BlockSpec(memory_space=pltpu.VMEM)
    hbm = pl.BlockSpec(memory_space=pl.ANY)
    dma = pltpu.SemaphoreType.DMA
    return pl.pallas_call(
        functools.partial(kernel, reps, owners),
        out_shape=jax.ShapeDtypeStruct((nodes, width), BF),
        in_specs=[hbm, hbm, smem, smem, smem, vmem, vmem, hbm, hbm],
        out_specs=vmem,
        scratch_shapes=[
            pltpu.VMEM((owners, 2 * halo), jnp.int32),
            pltpu.VMEM((nodes, width), BF),
            pltpu.VMEM((lines, nodes), BF),
            pltpu.VMEM((HOPS, owners, 2 * halo, width // 2), BF),
            pltpu.VMEM((HOPS, owners, 2 * halo, width // 2), BF),
            pltpu.VMEM((lines, width // 2), BF),
            pltpu.VMEM((side, 2 * side), BF),
            pltpu.VMEM((reps, slots, side, side), BF),
            pltpu.VMEM((reps, mark_lines, 128), F32),
            pltpu.VMEM((nodes, columns), BF),
            pltpu.VMEM((nodes, lines), BF),
            pltpu.VMEM((nodes, width), F32),
            pltpu.VMEM(w_in.shape, BF),
            pltpu.VMEM(w_out.shape, BF),
            dma((4,)),
            dma, dma, dma, dma,
            dma((HOPS,)),
            dma((HOPS,)),
            dma((HOPS,)),
        ],
        compiler_params=pltpu.CompilerParams(
            collective_id=0, has_side_effects=True, vmem_limit_bytes=60 * 1024 * 1024
        ),
    )(
        features, tiles[0, 0], tile_row[0, 0], tile_col[0, 0], tile_live[0], jnp.transpose(send_index[0]), gain, w_in, w_out
    )


def solution(mesh):
    placed = (
        P("rows", None),
        P("rows", "rep", None, None, None),
        P("rows", "rep", None),
        P("rows", "rep", None),
        P("rows", "rep"),
        P("rows", None, None),
        P(),
        P(),
        P(),
    )
    body = functools.partial(per_device, mesh.shape["rep"], mesh.shape["rows"])
    return jax.shard_map(body, mesh=mesh, in_specs=placed, out_specs=P("rows", None), check_vma=False)
```

time: 305 us -> 75.8 us (0.25)
  waiting for transfers between devices: 162 us -> 0 us
  blocking collectives: 82.1 us -> 0 us
  Pallas kernels: 0 us -> 73.2 us
  starting transfers between devices: 20.7 us -> 0 us
  between operations: 14.1 us -> 0.66 us
  local copies, waits for them, and re-layouts: 14.5 us -> 1.67 us
  matrix products: 4.75 us -> 0 us
  other arithmetic: 4.68 us -> 0 us
    psum x3 -> x0, waiting for transfers between devices: 141 us -> none  [per_device(): gathered = lax.psum(partial_value, 'rep')]
    all_to_all x2 -> x0, blocking collectives: 82.1 us -> none  [per_device(): lax.all_to_all(outgoing, 'rows', split_axis=0, concat_axis=0, tiled=True)]
    pallas_call x0 -> x1, Pallas kernels: none -> 73.2 us  [per_device(): pl.pallas_call(functools.partial(kernel, reps, owners), out_shape=jax.Sha...]
    all_to_all x1 -> x0, waiting for transfers between devices: 21 us -> none  [per_device(): lax.all_to_all(outgoing, 'rows', split_axis=0, concat_axis=0, tiled=True)]
    all_to_all x1 -> x0, starting transfers between devices: 20.6 us -> none  [per_device(): lax.all_to_all(outgoing, 'rows', split_axis=0, concat_axis=0, tiled=True)]
    gather x9 -> x0, local copies, waits for them, and re-layouts: 9.05 us -> none  [the longest x6 7.36 us: per_device(): outgoing = current[send_index[0]]]
    dot_general x9 -> x0, matrix products: 4.75 us -> none  [the longest x3 2.67 us: update_rows(): jnp.dot(inner, second, preferred_element_type=jnp.float32)]
    reduce_sum x3 -> x0, other arithmetic: 3.81 us -> none  [update_rows(): scale = lax.rsqrt(jnp.mean(mixed * mixed, axis=-1, keepdims=True) + 1e-06)]
  transfers between devices with their start and end apart: 4 -> 0, of which waited for: 4 -> 0; matrix products, arithmetic and copies ran while one was open for 0% -> 0% of each run, Pallas kernels for 0% -> 0%
where the time goes in v1:
time: 75.8 us; the launch traced here: 75.6 us
  Pallas kernels  73.2 us (97%)
  local copies, waits for them, and re-layouts  1.67 us (2%)
    pallas_call x1, Pallas kernels, per_device(): pl.pallas_call(functools.partial(kernel, reps, owners), out_shape=jax.Sha...  73.2 us
    unnamed x1, local copies, waits for them, and re-layouts  1.67 us

profile of v1, /device:TPU:1, one launch (start us, length us, event | category | flops | bytes accessed | tf_op | source)
XLA Modules:
  0.0 75.6 jit_solution(474676371543966992)
XLA Ops:
  0.7 73.2 %shard_map.91 = bf16[512,256]{1,0:T(8,128)(2,1)} custom-call(bf16[512,256]{1,0:T(8,128)(2,1)} %feat_hbm.1, bf16[2,256,256]{2,1,0:T(8,128)(2,1)} %bitcast.8, s32[2]{0:T(128)} %bitcast.10, s32[2]{0:T(128)} %bitcast.11, s32[1]{0:T(128)} %bitcast.7.live_ref, s32[4,128]{1,0:T(4,128)} %bitcast.9, f32[3,256]{1,0:T(4,128)} %gain_ref.1, ...), custom_call_target="tpu_custom_call" | custom-call | tf_op jit(solution)/shard_map/pallas_call | solution.py:227
  73.9 1.7 %copy.12 = bf16[512,256]{1,0:T(8,128)(2,1)} copy(bf16[512,256]{1,0:T(8,128)(2,1)} %shard_map.91) | data formatting | bytes 524288

commit v2 on v1

v2 whole, which is shorter than its diff:
```python
import functools

import jax
import jax.numpy as jnp
from jax import lax
from jax.experimental import pallas as pl
from jax.experimental.pallas import tpu as pltpu
from jax.sharding import PartitionSpec as P

HOPS = 3
DIRECT = 0
BATCHES = ((0, 3), (3, 7), (7, 11), (11, 16))
FOLDED_FIRST = True
MESH = pl.DeviceIdType.MESH
BF = jnp.bfloat16
F32 = jnp.float32


def plane_of(owners):
    return {128: (4, 16, 2), 8: (2, 2, 2), 4: (4, 1, 1)}[owners]


def batches_of(zs):
    if zs == 16:
        return DIRECT, BATCHES
    return min(1, zs - 1), ((min(1, zs - 1), zs),)


def kernel(
    reps, owners, feat_hbm, tiles_hbm, row_hbm, col_hbm, live_hbm, index_hbm, gain_hbm, win_hbm, wout_hbm,
    out_ref,
    row_ref, col_ref, live_ref, index_ref, gain_ref,
    index_t, cur, pick, sent, recv, half_mask, spread, tiles_all, marks, block, wide, total, win, wout,
    load_sem, tile_send, tile_recv, mark_send, mark_recv, halo_send, halo_recv, fold_send, fold_recv,
):
    ys, zs, cs = plane_of(owners)
    direct, batches = batches_of(zs)
    rep = lax.axis_index("rep")
    me = lax.axis_index("rows")
    my_y, my_z, my_c = me // (zs * cs), (me // cs) % zs, me % cs
    nodes, width = feat_hbm.shape
    side = tiles_hbm.shape[-1]
    slots = tiles_hbm.shape[0]
    halo = index_hbm.shape[0]
    half = width // 2
    group = 2 * halo
    row_tiles = nodes // side
    col_tiles = block.shape[1] // side
    own_tiles = nodes // side
    far_y = sorted(range(ys), key=lambda d: -min(d, ys - d))
    far_x = sorted(range(1, reps), key=lambda d: -min(d, reps - d))

    barrier = pltpu.get_barrier_semaphore()

    def at(sign, dz, dy, dc):
        y = lax.rem(my_y + sign * dy + ys, ys)
        z = lax.rem(my_z + sign * dz + zs, zs)
        c = lax.rem(my_c + sign * dc + cs, cs)
        return (y * zs + z) * cs + c

    def step_of(j):
        return zs // 2 + (1 - 2 * lax.rem(j, 2)) * ((j + 1) // 2)

    def my_dy(dz):
        return lax.rem(rep + ys * zs - dz, ys)

    def partners(sign, visit):
        def whole():
            @pl.loop(0, direct)
            def _(j):
                dz = step_of(j)
                for dy in far_y:
                    for dc in reversed(range(cs)):
                        visit(at(sign, dz, dy, dc), 0)

        if direct and not FOLDED_FIRST:
            whole()
        for b, (low, high) in enumerate(batches):
            if min(high, zs - 1) > low:

                @pl.loop(low, min(high, zs - 1))
                def _(j, b=b):
                    dz = step_of(j)
                    for dc in reversed(range(cs)):
                        visit(at(sign, dz, my_dy(dz), dc), b + 1)

        for dc in reversed(range(1, cs)):
            visit(at(sign, 0, my_dy(0), dc), len(batches))

        @pl.when(rep != 0)
        def _():
            visit(at(sign, 0, my_dy(0), 0), len(batches))

        if direct and FOLDED_FIRST:
            whole()

    def greet(owner, _):
        pl.semaphore_signal(barrier, inc=1, device_id=(rep, owner), device_id_type=MESH)

    partners(-1, greet)
    for d in far_x:
        pl.semaphore_signal(
            barrier, inc=1, device_id=(lax.rem(rep + d, reps), me), device_id_type=MESH
        )
    messages = direct * ys * cs + (zs - direct) * cs

    loads = [
        pltpu.make_async_copy(source, to, load_sem.at[n])
        for n, (source, to) in enumerate(
            (
                (index_hbm, index_ref), (feat_hbm, cur), (row_hbm, row_ref), (col_hbm, col_ref), (live_hbm, live_ref),
                (tiles_hbm, tiles_all.at[rep]), (gain_hbm, gain_ref), (win_hbm, win), (wout_hbm, wout),
            )
        )
    ]
    for load in loads:
        load.start()

    total_lines = owners * group
    lines = lax.broadcasted_iota(jnp.int32, (total_lines, half), 0)
    half_mask[...] = jnp.where(lax.rem(lines, group) < halo, 1.0, 0.0).astype(BF)
    x = lax.broadcasted_iota(jnp.int32, spread.shape, 0)
    y = lax.broadcasted_iota(jnp.int32, spread.shape, 1)
    same = (x // halo == y // group) & (lax.rem(x, halo) == lax.rem(y, halo))
    spread[...] = jnp.where(same, 1.0, 0.0).astype(BF)

    loads[0].wait()
    per = 16 // group
    index_t[...] = jnp.transpose(jnp.concatenate([index_ref[...]] * 2, axis=0))
    lane = lax.broadcasted_iota(jnp.int32, (group, group), 1)
    sub = lax.broadcasted_iota(jnp.int32, (group, group), 0)
    node = lax.broadcasted_iota(jnp.int32, (group, nodes), 1)
    for o in range(0, owners, per):
        rows = []
        for q in range(per):
            wanted = jnp.broadcast_to(index_t[o + q : o + q + 1, :], (group, group))
            wanted = jnp.sum(jnp.where(lane == sub, wanted, 0), axis=1, keepdims=True)
            rows.append(jnp.where(node == wanted, 1.0, 0.0).astype(F32))
        pick[o * group : (o + per) * group, :] = jnp.concatenate(rows, axis=0).astype(BF)

    loads[1].wait()

    def gather(hop):
        step = min(256, total_lines)
        for first in range(0, total_lines, step):
            got = jnp.dot(pick[first : first + step, :], cur[...], preferred_element_type=F32)
            line = lax.rem(lax.broadcasted_iota(jnp.int32, (step, half), 0), group)
            message = jnp.where(line < halo, got[:, :half], got[:, half:])
            sent[hop, first // group : (first + step) // group] = message.astype(BF).reshape(
                step // group, group, half
            )

    def exchange(hop):
        def send(owner, b):
            pltpu.make_async_remote_copy(
                src_ref=sent.at[hop, owner],
                dst_ref=recv.at[hop, me],
                send_sem=halo_send.at[hop],
                recv_sem=halo_recv.at[hop, b],
                device_id=(rep, owner),
                device_id_type=MESH,
            ).start()

        partners(1, send)

        @pl.when(rep == 0)
        def _():
            pltpu.make_async_copy(
                sent.at[hop, me], recv.at[hop, me], halo_recv.at[hop, len(batches)]
            ).start()

    def settle(ref, sem):
        pltpu.make_async_copy(ref, ref, sem).wait()

    def fold(hop, b):
        low, high = batches[b]
        settle(recv.at[hop, pl.ds(0, (high - low) * cs)], halo_recv.at[hop, b + 1])

        @pl.loop(low, high)
        def _(j):
            dz = step_of(j)
            y = lax.rem(my_y - my_dy(dz) + ys, ys)
            z = lax.rem(my_z - dz + zs, zs)
            pair = recv.at[hop, pl.ds((y * zs + z) * cs, cs)]
            for d in far_x:
                pltpu.make_async_remote_copy(
                    src_ref=pair,
                    dst_ref=pair,
                    send_sem=fold_send.at[hop],
                    recv_sem=fold_recv.at[hop],
                    device_id=(lax.rem(rep + d, reps), me),
                    device_id_type=MESH,
                ).start()

    def folded(hop):
        if direct:
            settle(recv.at[hop, pl.ds(0, direct * ys * cs)], halo_recv.at[hop, 0])
        settle(recv.at[hop, pl.ds(0, (reps - 1) * (zs - direct) * cs)], fold_recv.at[hop])

    gather(0)

    for load in loads[2:5]:
        load.wait()
    positions = row_tiles * col_tiles
    line = lax.broadcasted_iota(jnp.int32, marks.shape[1:], 0)
    mark = jnp.zeros(marks.shape[1:], F32)
    for slot in range(slots):
        where = row_ref[slot] * col_tiles + col_ref[slot]
        where = jnp.where(slot < live_ref[0, 0], where + slot * positions, -1)
        mark = jnp.where(line == where, 1.0, mark)
    marks[rep] = mark

    def place(source, slot, fresh=False):
        chunk = 128
        for r in range(row_tiles):
            for c in range(col_tiles):
                which = slot * positions + r * col_tiles + c
                here = marks[source, pl.ds(which, 1), :]
                here = jnp.concatenate([here] * (side // here.shape[1]), axis=1)
                here = jnp.broadcast_to(here, (16, side)).astype(BF)
                here = jnp.concatenate([here] * (chunk // 16), axis=0)
                for i in range(0, side, chunk):
                    value = tiles_all[source, slot, i : i + chunk, :] * here
                    to = (slice(r * side + i, r * side + i + chunk), slice(c * side, (c + 1) * side))
                    block[to] = value if fresh else block[to] + value

    loads[5].wait()
    place(rep, 0, fresh=True)
    place(rep, 1)

    def tile_to(d, source, slot, ref):
        pltpu.make_async_remote_copy(
            src_ref=ref.at[slot], dst_ref=tiles_all.at[source, slot], send_sem=tile_send,
            recv_sem=tile_recv.at[lax.rem(source - rep - d + 2 * reps, reps), slot],
            device_id=(lax.rem(rep + d, reps), me), device_id_type=MESH,
        ).start()

    pl.semaphore_wait(barrier, messages + reps - 1 - jnp.where(rep == 0, 1, 0))
    for d in far_x:
        pltpu.make_async_remote_copy(
            src_ref=marks.at[rep], dst_ref=marks.at[rep], send_sem=mark_send, recv_sem=mark_recv,
            device_id=(lax.rem(rep + d, reps), me), device_id_type=MESH,
        ).start()
    exchange(0)
    left, right = lax.rem(rep + reps - 1, reps), lax.rem(rep + 1, reps)
    tile_to(1, rep, 0, tiles_hbm)
    if reps == 2:
        tile_to(1, rep, 1, tiles_hbm)
    else:
        tile_to(reps - 1, rep, 1, tiles_hbm)
        tile_to(1, rep, 1, tiles_hbm)
        tile_to(reps - 1, rep, 0, tiles_hbm)

    for load in loads[6:]:
        load.wait()
    others = pl.ds(0, reps - 1)
    settle(marks.at[others], mark_recv)
    todo = list(reversed(range(len(batches))))
    if reps == 2:
        for slot in range(slots):
            settle(tiles_all.at[0, 0], tile_recv.at[1, slot])
            place(left, slot)
    else:
        settle(tiles_all.at[0, 0], tile_recv.at[reps - 1, 0])
        tile_to(1, left, 0, tiles_all.at[left])
        settle(tiles_all.at[0, 0], tile_recv.at[1, 1])
        tile_to(reps - 1, right, 1, tiles_all.at[right])
        for source, slot in ((left, 0), (right, 1)):
            if todo:
                fold(0, todo.pop(0))
            place(source, slot)
        for source, slot, n in ((left, 1, reps - 1), (right, 0, 1)):
            if todo:
                fold(0, todo.pop(0))
            settle(tiles_all.at[0, 0], tile_recv.at[n, slot])
            place(source, slot)
    for b in todo:
        fold(0, b)
    if reps == 4:
        for slot in range(slots):
            settle(tiles_all.at[0, 0], tile_recv.at[2, slot])
            place(lax.rem(rep + 2, reps), slot)
    for c in range(own_tiles, col_tiles):
        q = c - own_tiles
        columns = min(2 * side, wide.shape[1])
        wide[:, q * 2 * side : q * 2 * side + columns] = jnp.dot(
            block[:, c * side : (c + 1) * side], spread[:, :columns], preferred_element_type=F32
        ).astype(BF)

    def own_part():
        for first in range(0, nodes, rows):
            total[first : first + rows, :] = jnp.dot(
                block[first : first + rows, :nodes], cur[...], preferred_element_type=F32
            ) + cur[first : first + rows, :].astype(F32)

    rows = 256
    for hop in range(HOPS):
        if hop:
            gather(hop)
            exchange(hop)
        own_part()
        if hop:
            for b in reversed(range(len(batches))):
                fold(hop, b)
        folded(hop)
        came = recv[hop].reshape(total_lines, half)
        low = came * half_mask[...]
        both = jnp.concatenate([low, came - low], axis=1)
        for first in range(0, nodes, rows):
            here = slice(first, first + rows)
            mixed = total[here, :] + jnp.dot(wide[here, :], both, preferred_element_type=F32)
            scale = lax.rsqrt(jnp.mean(mixed * mixed, axis=-1, keepdims=True) + 1e-06)
            normed = (mixed * scale * gain_ref[hop : hop + 1, :]).astype(BF)
            inner = jax.nn.gelu(jnp.dot(normed, win[hop], preferred_element_type=F32)).astype(BF)
            result = (mixed + jnp.dot(inner, wout[hop], preferred_element_type=F32)).astype(BF)
            if hop == HOPS - 1:
                out_ref[here, :] = result
            else:
                cur[here, :] = result

    for hop in range(HOPS):

        @pl.when(rep == 0)
        def _(hop=hop):
            settle(sent.at[hop, pl.ds(0, messages - 1)], halo_send.at[hop])

        @pl.when(rep != 0)
        def _(hop=hop):
            settle(sent.at[hop, pl.ds(0, messages)], halo_send.at[hop])

        settle(recv.at[hop, pl.ds(0, (reps - 1) * (zs - direct) * cs)], fold_send.at[hop])
    settle(marks.at[others], mark_send)
    sent_tiles = tiles_all.at[others] if reps == 4 else tiles_all.at[pl.ds(0, 1)]
    settle(sent_tiles, tile_send)


def per_device(reps, owners, features, tiles, tile_row, tile_col, tile_live, send_index, gain, w_in, w_out):
    nodes, width = features.shape
    slots, side = tiles.shape[2], tiles.shape[-1]
    halo = send_index.shape[2]
    halo_pad = (owners * halo + side - 1) // side * side
    columns = nodes + halo_pad
    lines = owners * 2 * halo
    positions = (nodes // side) * (columns // side)
    mark_lines = (slots * positions + 7) // 8 * 8
    batches = len(batches_of(plane_of(owners)[1])[1])
    vmem = pl.BlockSpec(memory_space=pltpu.VMEM)
    hbm = pl.BlockSpec(memory_space=pltpu.HBM)
    dma = pltpu.SemaphoreType.DMA
    return pl.pallas_call(
        functools.partial(kernel, reps, owners),
        out_shape=pltpu.VMEM((nodes, width), BF),
        in_specs=[hbm] * 9,
        out_specs=vmem,
        scratch_shapes=[
            pltpu.SMEM((slots,), jnp.int32),
            pltpu.SMEM((slots,), jnp.int32),
            pltpu.SMEM((1, 1), jnp.int32),
            pltpu.VMEM((halo, owners), jnp.int32),
            pltpu.VMEM(gain.shape, F32),
            pltpu.VMEM((owners, 2 * halo), jnp.int32),
            pltpu.VMEM((nodes, width), BF),
            pltpu.VMEM((lines, nodes), BF),
            pltpu.VMEM((HOPS, owners, 2 * halo, width // 2), BF),
            pltpu.VMEM((HOPS, owners, 2 * halo, width // 2), BF),
            pltpu.VMEM((lines, width // 2), BF),
            pltpu.VMEM((side, 2 * side), BF),
            pltpu.VMEM((reps, slots, side, side), BF),
            pltpu.VMEM((reps, mark_lines, 128), F32),
            pltpu.VMEM((nodes, columns), BF),
            pltpu.VMEM((nodes, lines), BF),
            pltpu.VMEM((nodes, width), F32),
            pltpu.VMEM(w_in.shape, BF),
            pltpu.VMEM(w_out.shape, BF),
            dma((9,)),
            dma,
            dma((reps, slots)),
            dma,
            dma,
            dma((HOPS,)),
            dma((HOPS, batches + 1)),
            dma((HOPS,)),
            dma((HOPS,)),
        ],
        compiler_params=pltpu.CompilerParams(
            collective_id=0, has_side_effects=True, vmem_limit_bytes=63 * 1024 * 1024
        ),
    )(
        features, tiles[0, 0], tile_row[0, 0], tile_col[0, 0], tile_live, jnp.transpose(send_index[0]), gain, w_in, w_out
    )


def solution(mesh):
    placed = (
        P("rows", None),
        P("rows", "rep", None, None, None),
        P("rows", "rep", None),
        P("rows", "rep", None),
        P("rows", "rep"),
        P("rows", None, None),
        P(),
        P(),
        P(),
    )
    body = functools.partial(per_device, mesh.shape["rep"], mesh.shape["rows"])
    return jax.shard_map(body, mesh=mesh, in_specs=placed, out_specs=P("rows", None), check_vma=False)
```

time: 75.8 us -> 63.7 us (0.84)
  Pallas kernels: 73.2 us -> 62.2 us
  local copies, waits for them, and re-layouts: 1.67 us -> 0.71 us
    pallas_call x1, Pallas kernels: 73.2 us -> 62.2 us  [per_device(): pl.pallas_call(functools.partial(kernel, reps, owners), out_shape=pltpu.V...]
    unnamed x1, local copies, waits for them, and re-layouts: 1.67 us -> 0.71 us
where the time goes in v2:
time: 63.7 us; the launch traced here: 63.6 us
  Pallas kernels  62.2 us (98%)
  local copies, waits for them, and re-layouts  0.71 us (1%)
  between operations  0.66 us (1%)
    pallas_call x1, Pallas kernels, per_device(): pl.pallas_call(functools.partial(kernel, reps, owners), out_shape=pltpu.V...  62.2 us

profile of v2, /device:TPU:1, one launch (start us, length us, event | category | flops | bytes accessed | tf_op | source)
XLA Modules:
  0.0 63.6 jit_solution(4820498257496051828)
XLA Ops:
  0.7 62.2 %shard_map.91 = bf16[512,256]{1,0:T(8,128)(2,1)S(1)} custom-call(bf16[512,256]{1,0:T(8,128)(2,1)} %feat_hbm.1, bf16[2,256,256]{2,1,0:T(8,128)(2,1)} %bitcast.6, s32[2]{0:T(128)} %bitcast.8, s32[2]{0:T(128)} %bitcast.9, s32[1,1]{1,0:T(1,128)S(6)} %copy.12.live_hbm, s32[4,128]{1,0:T(4,128)} %bitcast.7, f32[3,256]{1,0:T(4,128)} %gain_hbm.1, ...), custom_call_target="tpu_custom_call" | custom-call | tf_op jit(solution)/shard_map/pallas_call | solution.py:350
  62.9 0.7 %copy.11 = bf16[512,256]{1,0:T(8,128)(2,1)} copy(bf16[512,256]{1,0:T(8,128)(2,1)S(1)} %shard_map.91) | data formatting | bytes 524288

commit v3 on v2

--- a/solution.py
+++ b/solution.py
@@ -8,22 +8,20 @@
 from jax.sharding import PartitionSpec as P
 
 HOPS = 3
-DIRECT = 0
-BATCHES = ((0, 3), (3, 7), (7, 11), (11, 16))
-FOLDED_FIRST = True
+ENDS = (0, 3, 7, 11, 16)
 MESH = pl.DeviceIdType.MESH
 BF = jnp.bfloat16
 F32 = jnp.float32
 
 
-def plane_of(owners):
-    return {128: (4, 16, 2), 8: (2, 2, 2), 4: (4, 1, 1)}[owners]
+def plane_of(reps, owners):
+    cores = 2 if owners >= 4 * reps else 1
+    return reps, owners // (reps * cores), cores
 
 
 def batches_of(zs):
-    if zs == 16:
-        return DIRECT, BATCHES
-    return min(1, zs - 1), ((min(1, zs - 1), zs),)
+    ends = ENDS if zs == ENDS[-1] else (0, zs)
+    return tuple(zip(ends[:-1], ends[1:]))
 
 
 def kernel(
@@ -33,8 +31,8 @@
     index_t, cur, pick, sent, recv, half_mask, spread, tiles_all, marks, block, wide, total, win, wout,
     load_sem, tile_send, tile_recv, mark_send, mark_recv, halo_send, halo_recv, fold_send, fold_recv,
 ):
-    ys, zs, cs = plane_of(owners)
-    direct, batches = batches_of(zs)
+    ys, zs, cs = plane_of(reps, owners)
+    batches = batches_of(zs)
     rep = lax.axis_index("rep")
     me = lax.axis_index("rows")
     my_y, my_z, my_c = me // (zs * cs), (me // cs) % zs, me % cs
@@ -65,16 +63,6 @@
         return lax.rem(rep + ys * zs - dz, ys)
 
     def partners(sign, visit):
-        def whole():
-            @pl.loop(0, direct)
-            def _(j):
-                dz = step_of(j)
-                for dy in far_y:
-                    for dc in reversed(range(cs)):
-                        visit(at(sign, dz, dy, dc), 0)
-
-        if direct and not FOLDED_FIRST:
-            whole()
         for b, (low, high) in enumerate(batches):
             if min(high, zs - 1) > low:
 
@@ -82,19 +70,19 @@
                 def _(j, b=b):
                     dz = step_of(j)
                     for dc in reversed(range(cs)):
-                        visit(at(sign, dz, my_dy(dz), dc), b + 1)
-
+                        visit(at(sign, dz, my_dy(dz), dc), j * 2 + dc, b)
+
+        base = (zs - 1) * 2
         for dc in reversed(range(1, cs)):
-            visit(at(sign, 0, my_dy(0), dc), len(batches))
+            visit(at(sign, 0, my_dy(0), dc), base + dc, len(batches) - 1)
 
         @pl.when(rep != 0)
         def _():
-            visit(at(sign, 0, my_dy(0), 0), len(batches))
-
-        if direct and FOLDED_FIRST:
-            whole()
-
-    def greet(owner, _):
+            visit(at(sign, 0, my_dy(0), 0), base, len(batches) - 1)
+
+    messages = zs * cs
+
+    def greet(owner, place, b):
         pl.semaphore_signal(barrier, inc=1, device_id=(rep, owner), device_id_type=MESH)
 
     partners(-1, greet)
@@ -102,7 +90,6 @@
         pl.semaphore_signal(
             barrier, inc=1, device_id=(lax.rem(rep + d, reps), me), device_id_type=MESH
         )
-    messages = direct * ys * cs + (zs - direct) * cs
 
     loads = [
         pltpu.make_async_copy(source, to, load_sem.at[n])
@@ -116,33 +103,30 @@
     for load in loads:
         load.start()
 
-    total_lines = owners * group
-    lines = lax.broadcasted_iota(jnp.int32, (total_lines, half), 0)
-    half_mask[...] = jnp.where(lax.rem(lines, group) < halo, 1.0, 0.0).astype(BF)
-    x = lax.broadcasted_iota(jnp.int32, spread.shape, 0)
-    y = lax.broadcasted_iota(jnp.int32, spread.shape, 1)
-    same = (x // halo == y // group) & (lax.rem(x, halo) == lax.rem(y, halo))
-    spread[...] = jnp.where(same, 1.0, 0.0).astype(BF)
-
     loads[0].wait()
-    per = 16 // group
     index_t[...] = jnp.transpose(jnp.concatenate([index_ref[...]] * 2, axis=0))
     lane = lax.broadcasted_iota(jnp.int32, (group, group), 1)
     sub = lax.broadcasted_iota(jnp.int32, (group, group), 0)
     node = lax.broadcasted_iota(jnp.int32, (group, nodes), 1)
-    for o in range(0, owners, per):
-        rows = []
-        for q in range(per):
-            wanted = jnp.broadcast_to(index_t[o + q : o + q + 1, :], (group, group))
-            wanted = jnp.sum(jnp.where(lane == sub, wanted, 0), axis=1, keepdims=True)
-            rows.append(jnp.where(node == wanted, 1.0, 0.0).astype(F32))
-        pick[o * group : (o + per) * group, :] = jnp.concatenate(rows, axis=0).astype(BF)
+
+    def choose(owner):
+        wanted = jnp.broadcast_to(index_t[pl.ds(owner, 1), :], (group, group))
+        wanted = jnp.sum(jnp.where(lane == sub, wanted, 0), axis=1, keepdims=True)
+        return jnp.where(node == wanted, 1.0, 0.0).astype(F32)
+
+    for j in range(zs):
+        dz = step_of(jnp.int32(j))
+        rows = [choose(at(1, dz, my_dy(dz), dc)) for dc in range(cs)]
+        rows += [rows[-1]] * (2 - cs)
+        pick[j * 2 * group : (j + 1) * 2 * group, :] = jnp.concatenate(rows, axis=0).astype(BF)
 
     loads[1].wait()
 
     def gather(hop):
-        step = min(256, total_lines)
-        for first in range(0, total_lines, step):
+        got_lines = zs * 2 * group
+        step = 256
+        for first in range(0, got_lines, step):
+            step = min(step, got_lines - first)
             got = jnp.dot(pick[first : first + step, :], cur[...], preferred_element_type=F32)
             line = lax.rem(lax.broadcasted_iota(jnp.int32, (step, half), 0), group)
             message = jnp.where(line < halo, got[:, :half], got[:, half:])
@@ -151,9 +135,9 @@
             )
 
     def exchange(hop):
-        def send(owner, b):
+        def send(owner, place, b):
             pltpu.make_async_remote_copy(
-                src_ref=sent.at[hop, owner],
+                src_ref=sent.at[hop, place],
                 dst_ref=recv.at[hop, me],
                 send_sem=halo_send.at[hop],
                 recv_sem=halo_recv.at[hop, b],
@@ -166,7 +150,7 @@
         @pl.when(rep == 0)
         def _():
             pltpu.make_async_copy(
-                sent.at[hop, me], recv.at[hop, me], halo_recv.at[hop, len(batches)]
+                sent.at[hop, (zs - 1) * 2], recv.at[hop, me], halo_recv.at[hop, len(batches) - 1]
             ).start()
 
     def settle(ref, sem):
@@ -174,7 +158,7 @@
 
     def fold(hop, b):
         low, high = batches[b]
-        settle(recv.at[hop, pl.ds(0, (high - low) * cs)], halo_recv.at[hop, b + 1])
+        settle(recv.at[hop, pl.ds(0, (high - low) * cs)], halo_recv.at[hop, b])
 
         @pl.loop(low, high)
         def _(j):
@@ -192,10 +176,18 @@
                     device_id_type=MESH,
                 ).start()
 
-    def folded(hop):
-        if direct:
-            settle(recv.at[hop, pl.ds(0, direct * ys * cs)], halo_recv.at[hop, 0])
-        settle(recv.at[hop, pl.ds(0, (reps - 1) * (zs - direct) * cs)], fold_recv.at[hop])
+    folds = (reps - 1) * messages
+
+    def finish_sends(hop):
+        @pl.when(rep == 0)
+        def _():
+            settle(sent.at[hop, pl.ds(0, messages - 1)], halo_send.at[hop])
+
+        @pl.when(rep != 0)
+        def _():
+            settle(sent.at[hop, pl.ds(0, messages)], halo_send.at[hop])
+
+        settle(recv.at[hop, pl.ds(0, folds)], fold_send.at[hop])
 
     gather(0)
 
@@ -224,10 +216,6 @@
                     to = (slice(r * side + i, r * side + i + chunk), slice(c * side, (c + 1) * side))
                     block[to] = value if fresh else block[to] + value
 
-    loads[5].wait()
-    place(rep, 0, fresh=True)
-    place(rep, 1)
-
     def tile_to(d, source, slot, ref):
         pltpu.make_async_remote_copy(
             src_ref=ref.at[slot], dst_ref=tiles_all.at[source, slot], send_sem=tile_send,
@@ -235,14 +223,13 @@
             device_id=(lax.rem(rep + d, reps), me), device_id_type=MESH,
         ).start()
 
+    left, right = lax.rem(rep + reps - 1, reps), lax.rem(rep + 1, reps)
     pl.semaphore_wait(barrier, messages + reps - 1 - jnp.where(rep == 0, 1, 0))
     for d in far_x:
         pltpu.make_async_remote_copy(
             src_ref=marks.at[rep], dst_ref=marks.at[rep], send_sem=mark_send, recv_sem=mark_recv,
             device_id=(lax.rem(rep + d, reps), me), device_id_type=MESH,
         ).start()
-    exchange(0)
-    left, right = lax.rem(rep + reps - 1, reps), lax.rem(rep + 1, reps)
     tile_to(1, rep, 0, tiles_hbm)
     if reps == 2:
         tile_to(1, rep, 1, tiles_hbm)
@@ -250,6 +237,19 @@
         tile_to(reps - 1, rep, 1, tiles_hbm)
         tile_to(1, rep, 1, tiles_hbm)
         tile_to(reps - 1, rep, 0, tiles_hbm)
+    exchange(0)
+
+    total_lines = owners * group
+    lines = lax.broadcasted_iota(jnp.int32, (total_lines, half), 0)
+    half_mask[...] = jnp.where(lax.rem(lines, group) < halo, 1.0, 0.0).astype(BF)
+    x = lax.broadcasted_iota(jnp.int32, spread.shape, 0)
+    y = lax.broadcasted_iota(jnp.int32, spread.shape, 1)
+    same = (x // halo == y // group) & (lax.rem(x, halo) == lax.rem(y, halo))
+    spread[...] = jnp.where(same, 1.0, 0.0).astype(BF)
+
+    loads[5].wait()
+    place(rep, 0, fresh=True)
+    place(rep, 1)
 
     for load in loads[6:]:
         load.wait()
@@ -302,36 +302,31 @@
         if hop:
             for b in reversed(range(len(batches))):
                 fold(hop, b)
-        folded(hop)
+            finish_sends(hop - 1)
+        if hop == HOPS - 1:
+            settle(marks.at[others], mark_send)
+            settle(tiles_all.at[others] if reps == 4 else tiles_all.at[pl.ds(0, 1)], tile_send)
+        settle(recv.at[hop, pl.ds(0, folds)], fold_recv.at[hop])
         came = recv[hop].reshape(total_lines, half)
         low = came * half_mask[...]
         both = jnp.concatenate([low, came - low], axis=1)
-        for first in range(0, nodes, rows):
-            here = slice(first, first + rows)
-            mixed = total[here, :] + jnp.dot(wide[here, :], both, preferred_element_type=F32)
-            scale = lax.rsqrt(jnp.mean(mixed * mixed, axis=-1, keepdims=True) + 1e-06)
-            normed = (mixed * scale * gain_ref[hop : hop + 1, :]).astype(BF)
-            inner = jax.nn.gelu(jnp.dot(normed, win[hop], preferred_element_type=F32)).astype(BF)
-            result = (mixed + jnp.dot(inner, wout[hop], preferred_element_type=F32)).astype(BF)
+        parts = [slice(first, first + rows) for first in range(0, nodes, rows)]
+        mixed, normed, inner = [], [], []
+        for here in parts:
+            mixed.append(total[here, :] + jnp.dot(wide[here, :], both, preferred_element_type=F32))
+        for value in mixed:
+            scale = lax.rsqrt(jnp.mean(value * value, axis=-1, keepdims=True) + 1e-06)
+            normed.append((value * scale * gain_ref[hop : hop + 1, :]).astype(BF))
+        for value in normed:
+            inner.append(jax.nn.gelu(jnp.dot(value, win[hop], preferred_element_type=F32)).astype(BF))
+        for n, here in enumerate(parts):
+            result = mixed[n] + jnp.dot(inner[n], wout[hop], preferred_element_type=F32)
             if hop == HOPS - 1:
-                out_ref[here, :] = result
+                out_ref[here, :] = result.astype(BF)
             else:
-                cur[here, :] = result
-
-    for hop in range(HOPS):
-
-        @pl.when(rep == 0)
-        def _(hop=hop):
-            settle(sent.at[hop, pl.ds(0, messages - 1)], halo_send.at[hop])
-
-        @pl.when(rep != 0)
-        def _(hop=hop):
-            settle(sent.at[hop, pl.ds(0, messages)], halo_send.at[hop])
-
-        settle(recv.at[hop, pl.ds(0, (reps - 1) * (zs - direct) * cs)], fold_send.at[hop])
-    settle(marks.at[others], mark_send)
-    sent_tiles = tiles_all.at[others] if reps == 4 else tiles_all.at[pl.ds(0, 1)]
-    settle(sent_tiles, tile_send)
+                cur[here, :] = result.astype(BF)
+
+    finish_sends(HOPS - 1)
 
 
 def per_device(reps, owners, features, tiles, tile_row, tile_col, tile_live, send_index, gain, w_in, w_out):
@@ -343,14 +338,16 @@
     lines = owners * 2 * halo
     positions = (nodes // side) * (columns // side)
     mark_lines = (slots * positions + 7) // 8 * 8
-    batches = len(batches_of(plane_of(owners)[1])[1])
+    _, zs, _ = plane_of(reps, owners)
+    batches = len(batches_of(zs))
+    pieces = zs * 2
     vmem = pl.BlockSpec(memory_space=pltpu.VMEM)
     hbm = pl.BlockSpec(memory_space=pltpu.HBM)
     dma = pltpu.SemaphoreType.DMA
     return pl.pallas_call(
         functools.partial(kernel, reps, owners),
         out_shape=pltpu.VMEM((nodes, width), BF),
-        in_specs=[hbm] * 9,
+        in_specs=[hbm] * 4 + [pl.BlockSpec(memory_space=pl.ANY)] + [hbm] * 4,
         out_specs=vmem,
         scratch_shapes=[
             pltpu.SMEM((slots,), jnp.int32),
@@ -360,8 +357,8 @@
             pltpu.VMEM(gain.shape, F32),
             pltpu.VMEM((owners, 2 * halo), jnp.int32),
             pltpu.VMEM((nodes, width), BF),
-            pltpu.VMEM((lines, nodes), BF),
-            pltpu.VMEM((HOPS, owners, 2 * halo, width // 2), BF),
+            pltpu.VMEM((pieces * 2 * halo, nodes), BF),
+            pltpu.VMEM((HOPS, pieces, 2 * halo, width // 2), BF),
             pltpu.VMEM((HOPS, owners, 2 * halo, width // 2), BF),
             pltpu.VMEM((lines, width // 2), BF),
             pltpu.VMEM((side, 2 * side), BF),
@@ -378,7 +375,7 @@
             dma,
             dma,
             dma((HOPS,)),
-            dma((HOPS, batches + 1)),
+            dma((HOPS, batches)),
             dma((HOPS,)),
             dma((HOPS,)),
         ],

time: 63.7 us -> 61.3 us (0.962)
  Pallas kernels: 62.2 us -> 59.8 us
    pallas_call x1, Pallas kernels: 62.2 us -> 59.8 us  [per_device(): pl.pallas_call(functools.partial(kernel, reps, owners), out_shape=pltpu.V...]
where the time goes in v3:
time: 61.3 us; the launch traced here: 61.2 us
  Pallas kernels  59.8 us (98%)
  local copies, waits for them, and re-layouts  0.71 us (1%)
  between operations  0.66 us (1%)
    pallas_call x1, Pallas kernels, per_device(): pl.pallas_call(functools.partial(kernel, reps, owners), out_shape=pltpu.V...  59.8 us

profile of v3, /device:TPU:1, one launch (start us, length us, event | category | flops | bytes accessed | tf_op | source)
XLA Modules:
  0.0 61.2 jit_solution(13077832273019610210)
XLA Ops:
  0.7 59.8 %shard_map.91 = bf16[512,256]{1,0:T(8,128)(2,1)S(1)} custom-call(bf16[512,256]{1,0:T(8,128)(2,1)} %feat_hbm.1, bf16[2,256,256]{2,1,0:T(8,128)(2,1)} %bitcast.6, s32[2]{0:T(128)} %bitcast.8, s32[2]{0:T(128)} %bitcast.9, s32[1,1]{1,0:T(1,128)S(6)} %copy.12.live_hbm, s32[4,128]{1,0:T(4,128)} %bitcast.7, f32[3,256]{1,0:T(4,128)} %gain_hbm.1, ...), custom_call_target="tpu_custom_call" | custom-call | tf_op jit(solution)/shard_map/pallas_call | solution.py:347
  60.5 0.7 %copy.11 = bf16[512,256]{1,0:T(8,128)(2,1)} copy(bf16[512,256]{1,0:T(8,128)(2,1)S(1)} %shard_map.91) | data formatting | bytes 524288

commit v4 on v3

--- a/solution.py
+++ b/solution.py
@@ -8,7 +8,7 @@
 from jax.sharding import PartitionSpec as P
 
 HOPS = 3
-ENDS = (0, 3, 7, 11, 16)
+ENDS = ((0, 3, 9), (0, 3, 7, 13), (0, 3, 7, 13))
 MESH = pl.DeviceIdType.MESH
 BF = jnp.bfloat16
 F32 = jnp.float32
@@ -20,8 +20,8 @@
 
 
 def batches_of(zs):
-    ends = ENDS if zs == ENDS[-1] else (0, zs)
-    return tuple(zip(ends[:-1], ends[1:]))
+    every = ENDS if zs == 16 else ((0, zs - 1),) * HOPS
+    return [tuple(zip(ends[:-1], ends[1:])) for ends in every]
 
 
 def kernel(
@@ -33,6 +33,8 @@
 ):
     ys, zs, cs = plane_of(reps, owners)
     batches = batches_of(zs)
+    near = [groups[-1][1] for groups in batches]
+    nearest = min(near)
     rep = lax.axis_index("rep")
     me = lax.axis_index("rows")
     my_y, my_z, my_c = me // (zs * cs), (me // cs) % zs, me % cs
@@ -62,30 +64,47 @@
     def my_dy(dz):
         return lax.rem(rep + ys * zs - dz, ys)
 
-    def partners(sign, visit):
-        for b, (low, high) in enumerate(batches):
-            if min(high, zs - 1) > low:
-
-                @pl.loop(low, min(high, zs - 1))
-                def _(j, b=b):
-                    dz = step_of(j)
+    def place_of(j, more):
+        return 2 * (zs + (zs - 1 - j) * (ys - 1) + more - 1 if more else j)
+
+    def partners(sign, hop, visit):
+        for b, (low, high) in enumerate(batches[hop]):
+
+            @pl.loop(low, high)
+            def _(j, b=b):
+                dz = step_of(j)
+                for dc in reversed(range(cs)):
+                    visit(at(sign, dz, my_dy(dz), dc), place_of(j, 0) + dc, b)
+
+        last = len(batches[hop])
+        if near[hop] < zs - 1:
+
+            @pl.loop(near[hop], zs - 1)
+            def _(j):
+                dz = step_of(j)
+                for more in range(ys):
                     for dc in reversed(range(cs)):
-                        visit(at(sign, dz, my_dy(dz), dc), j * 2 + dc, b)
-
-        base = (zs - 1) * 2
-        for dc in reversed(range(1, cs)):
-            visit(at(sign, 0, my_dy(0), dc), base + dc, len(batches) - 1)
-
-        @pl.when(rep != 0)
-        def _():
-            visit(at(sign, 0, my_dy(0), 0), base, len(batches) - 1)
-
-    messages = zs * cs
+                        owner = at(sign, dz, lax.rem(my_dy(dz) + more, ys), dc)
+                        visit(owner, place_of(j, more) + dc, last)
+
+        for more in range(ys):
+            dy = lax.rem(my_dy(0) + more, ys)
+            for dc in reversed(range(1, cs)):
+                visit(at(sign, 0, dy, dc), place_of(zs - 1, more) + dc, last)
+
+            @pl.when(dy != 0)
+            def _(dy=dy, more=more):
+                visit(at(sign, 0, dy, 0), place_of(zs - 1, more), last)
+
+    def messages(hop):
+        return (near[hop] + (zs - near[hop]) * ys) * cs - 1
+
+    widest = near.index(nearest)
 
     def greet(owner, place, b):
         pl.semaphore_signal(barrier, inc=1, device_id=(rep, owner), device_id_type=MESH)
 
-    partners(-1, greet)
+    partners(-1, widest, greet)
     for d in far_x:
         pl.semaphore_signal(
             barrier, inc=1, device_id=(lax.rem(rep + d, reps), me), device_id_type=MESH
@@ -116,14 +135,17 @@
 
     for j in range(zs):
         dz = step_of(jnp.int32(j))
-        rows = [choose(at(1, dz, my_dy(dz), dc)) for dc in range(cs)]
-        rows += [rows[-1]] * (2 - cs)
-        pick[j * 2 * group : (j + 1) * 2 * group, :] = jnp.concatenate(rows, axis=0).astype(BF)
+        for more in range(ys if j >= nearest else 1):
+            dy = lax.rem(my_dy(dz) + more, ys)
+            rows = [choose(at(1, dz, dy, dc)) for dc in range(cs)]
+            rows += [rows[-1]] * (2 - cs)
+            to = place_of(j, more) * group
+            pick[to : to + 2 * group, :] = jnp.concatenate(rows, axis=0).astype(BF)
 
     loads[1].wait()
 
     def gather(hop):
-        got_lines = zs * 2 * group
+        got_lines = (zs + (zs - near[hop]) * (ys - 1)) * 2 * group
         step = 256
         for first in range(0, got_lines, step):
             step = min(step, got_lines - first)
@@ -145,19 +167,22 @@
                 device_id_type=MESH,
             ).start()
 
-        partners(1, send)
-
-        @pl.when(rep == 0)
-        def _():
-            pltpu.make_async_copy(
-                sent.at[hop, (zs - 1) * 2], recv.at[hop, me], halo_recv.at[hop, len(batches) - 1]
-            ).start()
+        partners(1, hop, send)
+
+        for more in range(ys):
+
+            @pl.when(lax.rem(my_dy(0) + more, ys) == 0)
+            def _(more=more):
+                pltpu.make_async_copy(
+                    sent.at[hop, place_of(zs - 1, more)], recv.at[hop, me],
+                    halo_recv.at[hop, len(batches[hop])],
+                ).start()
 
     def settle(ref, sem):
         pltpu.make_async_copy(ref, ref, sem).wait()
 
     def fold(hop, b):
-        low, high = batches[b]
+        low, high = batches[hop][b]
         settle(recv.at[hop, pl.ds(0, (high - low) * cs)], halo_recv.at[hop, b])
 
         @pl.loop(low, high)
@@ -176,18 +201,12 @@
                     device_id_type=MESH,
                 ).start()
 
-    folds = (reps - 1) * messages
+    def folds(hop):
+        return (reps - 1) * near[hop] * cs
 
     def finish_sends(hop):
-        @pl.when(rep == 0)
-        def _():
-            settle(sent.at[hop, pl.ds(0, messages - 1)], halo_send.at[hop])
-
-        @pl.when(rep != 0)
-        def _():
-            settle(sent.at[hop, pl.ds(0, messages)], halo_send.at[hop])
-
-        settle(recv.at[hop, pl.ds(0, folds)], fold_send.at[hop])
+        settle(recv.at[hop, pl.ds(0, messages(hop))], halo_send.at[hop])
+        settle(recv.at[hop, pl.ds(0, folds(hop))], fold_send.at[hop])
 
     gather(0)
 
@@ -224,7 +243,7 @@
         ).start()
 
     left, right = lax.rem(rep + reps - 1, reps), lax.rem(rep + 1, reps)
-    pl.semaphore_wait(barrier, messages + reps - 1 - jnp.where(rep == 0, 1, 0))
+    pl.semaphore_wait(barrier, messages(widest) + reps - 1)
     for d in far_x:
         pltpu.make_async_remote_copy(
             src_ref=marks.at[rep], dst_ref=marks.at[rep], send_sem=mark_send, recv_sem=mark_recv,
@@ -255,7 +274,7 @@
         load.wait()
     others = pl.ds(0, reps - 1)
     settle(marks.at[others], mark_recv)
-    todo = list(reversed(range(len(batches))))
+    todo = list(reversed(range(len(batches[0]))))
     if reps == 2:
         for slot in range(slots):
             settle(tiles_all.at[0, 0], tile_recv.at[1, slot])
@@ -300,13 +319,14 @@
             exchange(hop)
         own_part()
         if hop:
-            for b in reversed(range(len(batches))):
+            for b in reversed(range(len(batches[hop]))):
                 fold(hop, b)
             finish_sends(hop - 1)
         if hop == HOPS - 1:
             settle(marks.at[others], mark_send)
             settle(tiles_all.at[others] if reps == 4 else tiles_all.at[pl.ds(0, 1)], tile_send)
-        settle(recv.at[hop, pl.ds(0, folds)], fold_recv.at[hop])
+        settle(recv.at[hop, pl.ds(0, (zs - near[hop]) * ys * cs)], halo_recv.at[hop, len(batches[hop])])
+        settle(recv.at[hop, pl.ds(0, folds(hop))], fold_recv.at[hop])
         came = recv[hop].reshape(total_lines, half)
         low = came * half_mask[...]
         both = jnp.concatenate([low, came - low], axis=1)
@@ -338,9 +358,10 @@
     lines = owners * 2 * halo
     positions = (nodes // side) * (columns // side)
     mark_lines = (slots * positions + 7) // 8 * 8
-    _, zs, _ = plane_of(reps, owners)
-    batches = len(batches_of(zs))
-    pieces = zs * 2
+    ys, zs, _ = plane_of(reps, owners)
+    groups = batches_of(zs)
+    batches = max(len(g) for g in groups) + 1
+    pieces = (zs + (zs - min(g[-1][1] for g in groups)) * (ys - 1)) * 2
     vmem = pl.BlockSpec(memory_space=pltpu.VMEM)
     hbm = pl.BlockSpec(memory_space=pltpu.HBM)
     dma = pltpu.SemaphoreType.DMA

time: 61.3 us -> 60.6 us (0.989)
  Pallas kernels: 59.8 us -> 59.1 us
    pallas_call x1, Pallas kernels: 59.8 us -> 59.1 us  [per_device(): pl.pallas_call(functools.partial(kernel, reps, owners), out_shape=pltpu.V...]
where the time goes in v4:
time: 60.6 us; the launch traced here: 60.5 us
  Pallas kernels  59.1 us (98%)
  local copies, waits for them, and re-layouts  0.71 us (1%)
  between operations  0.66 us (1%)
    pallas_call x1, Pallas kernels, per_device(): pl.pallas_call(functools.partial(kernel, reps, owners), out_shape=pltpu.V...  59.1 us

profile of v4, /device:TPU:1, one launch (start us, length us, event | category | flops | bytes accessed | tf_op | source)
XLA Modules:
  0.0 60.5 jit_solution(9217859923643900779)
XLA Ops:
  0.7 59.1 %shard_map.91 = bf16[512,256]{1,0:T(8,128)(2,1)S(1)} custom-call(bf16[512,256]{1,0:T(8,128)(2,1)} %feat_hbm.1, bf16[2,256,256]{2,1,0:T(8,128)(2,1)} %bitcast.6, s32[2]{0:T(128)} %bitcast.8, s32[2]{0:T(128)} %bitcast.9, s32[1,1]{1,0:T(1,128)S(6)} %copy.12.live_hbm, s32[4,128]{1,0:T(4,128)} %bitcast.7, f32[3,256]{1,0:T(4,128)} %gain_hbm.1, ...), custom_call_target="tpu_custom_call" | custom-call | tf_op jit(solution)/shard_map/pallas_call | solution.py:368
  59.8 0.7 %copy.11 = bf16[512,256]{1,0:T(8,128)(2,1)} copy(bf16[512,256]{1,0:T(8,128)(2,1)S(1)} %shard_map.91) | data formatting | bytes 524288

commit v5 on v4

--- a/solution.py
+++ b/solution.py
@@ -8,7 +8,7 @@
 from jax.sharding import PartitionSpec as P
 
 HOPS = 3
-ENDS = ((0, 3, 9), (0, 3, 7, 13), (0, 3, 7, 13))
+ENDS = ((0, 3, 7), (0, 3, 7, 13), (0, 3, 7, 13))
 MESH = pl.DeviceIdType.MESH
 BF = jnp.bfloat16
 F32 = jnp.float32
@@ -235,12 +235,20 @@
                     to = (slice(r * side + i, r * side + i + chunk), slice(c * side, (c + 1) * side))
                     block[to] = value if fresh else block[to] + value
 
-    def tile_to(d, source, slot, ref):
+    def tile_piece(d, source, slot, ref, piece):
+        cut = pl.ds(piece * (side // 2), side // 2)
         pltpu.make_async_remote_copy(
-            src_ref=ref.at[slot], dst_ref=tiles_all.at[source, slot], send_sem=tile_send,
-            recv_sem=tile_recv.at[lax.rem(source - rep - d + 2 * reps, reps), slot],
+            src_ref=ref.at[slot, cut], dst_ref=tiles_all.at[source, slot, cut], send_sem=tile_send,
+            recv_sem=tile_recv.at[lax.rem(source - rep - d + 2 * reps, reps), slot, piece],
             device_id=(lax.rem(rep + d, reps), me), device_id_type=MESH,
         ).start()
+
+    def tile_to(d, source, slot, ref):
+        for piece in range(2):
+            tile_piece(d, source, slot, ref, piece)
+
+    def await_piece(n, slot, piece):
+        settle(tiles_all.at[0, 0, pl.ds(0, side // 2)], tile_recv.at[n, slot, piece])
 
     left, right = lax.rem(rep + reps - 1, reps), lax.rem(rep + 1, reps)
     pl.semaphore_wait(barrier, messages(widest) + reps - 1)
@@ -277,13 +285,15 @@
     todo = list(reversed(range(len(batches[0]))))
     if reps == 2:
         for slot in range(slots):
-            settle(tiles_all.at[0, 0], tile_recv.at[1, slot])
+            await_piece(1, slot, 0)
+            await_piece(1, slot, 1)
             place(left, slot)
     else:
-        settle(tiles_all.at[0, 0], tile_recv.at[reps - 1, 0])
-        tile_to(1, left, 0, tiles_all.at[left])
-        settle(tiles_all.at[0, 0], tile_recv.at[1, 1])
-        tile_to(reps - 1, right, 1, tiles_all.at[right])
+        for piece in range(2):
+            await_piece(reps - 1, 0, piece)
+            tile_piece(1, left, 0, tiles_all.at[left], piece)
+            await_piece(1, 1, piece)
+            tile_piece(reps - 1, right, 1, tiles_all.at[right], piece)
         for source, slot in ((left, 0), (right, 1)):
             if todo:
                 fold(0, todo.pop(0))
@@ -291,13 +301,15 @@
         for source, slot, n in ((left, 1, reps - 1), (right, 0, 1)):
             if todo:
                 fold(0, todo.pop(0))
-            settle(tiles_all.at[0, 0], tile_recv.at[n, slot])
+            await_piece(n, slot, 0)
+            await_piece(n, slot, 1)
             place(source, slot)
     for b in todo:
         fold(0, b)
     if reps == 4:
         for slot in range(slots):
-            settle(tiles_all.at[0, 0], tile_recv.at[2, slot])
+            await_piece(2, slot, 0)
+            await_piece(2, slot, 1)
             place(lax.rem(rep + 2, reps), slot)
     for c in range(own_tiles, col_tiles):
         q = c - own_tiles
@@ -392,7 +404,7 @@
             pltpu.VMEM(w_out.shape, BF),
             dma((9,)),
             dma,
-            dma((reps, slots)),
+            dma((reps, slots, 2)),
             dma,
             dma,
             dma((HOPS,)),

time: 60.6 us -> 60.2 us (level)
  no operation moved by 1% of the time
where the time goes in v5:
time: 60.2 us; the launch traced here: 60.1 us
  Pallas kernels  58.7 us (98%)
  local copies, waits for them, and re-layouts  0.71 us (1%)
  between operations  0.66 us (1%)
    pallas_call x1, Pallas kernels, per_device(): pl.pallas_call(functools.partial(kernel, reps, owners), out_shape=pltpu.V...  58.7 us

profile of v5, /device:TPU:1, one launch (start us, length us, event | category | flops | bytes accessed | tf_op | source)
XLA Modules:
  0.0 60.1 jit_solution(1357980323016296114)
XLA Ops:
  0.7 58.7 %shard_map.91 = bf16[512,256]{1,0:T(8,128)(2,1)S(1)} custom-call(bf16[512,256]{1,0:T(8,128)(2,1)} %feat_hbm.1, bf16[2,256,256]{2,1,0:T(8,128)(2,1)} %bitcast.6, s32[2]{0:T(128)} %bitcast.8, s32[2]{0:T(128)} %bitcast.9, s32[1,1]{1,0:T(1,128)S(6)} %copy.12.live_hbm, s32[4,128]{1,0:T(4,128)} %bitcast.7, f32[3,256]{1,0:T(4,128)} %gain_hbm.1, ...), custom_call_target="tpu_custom_call" | custom-call | tf_op jit(solution)/shard_map/pallas_call | solution.py:380
  59.4 0.7 %copy.11 = bf16[512,256]{1,0:T(8,128)(2,1)} copy(bf16[512,256]{1,0:T(8,128)(2,1)S(1)} %shard_map.91) | data formatting | bytes 524288
